TPU v7x, 256 devices: a whole 4x4x8 slice. The times are simulated.
256 devices in a mesh: scen: 32 (over z, y), tile: 8 (over x, core).
Axes of the slice: x: 4, y: 4, z: 8, core: 2. Of those that a mesh axis runs over, the one named last changes fastest.
Arguments:
- factor_inv: bfloat16 [256, 768, 768], P('scen'), may hold values from -0.21875 to 0.21875
- pattern: int32 [256, 6, 6], P('scen'), may hold values 0 or 1
- border: bfloat16 [256, 768, 1024], P('scen', None, 'tile'), may hold values from -0.59765625 to 0.59765625
- row_scale: float32 [256, 768], P('scen'), may hold values from 0.25 to 4
- link_ids: int32 [256, 8], P('scen'), may hold values from 0 to 63, as said below
- first_diag: float32 [8192], replicated, may hold values from 10 to 100
Outputs:
- schur: float32 [8192, 8192], P('tile', 'scen')
Inputs may be any that keep to these rules, and one draw needn't show every extreme that they name: link_ids[s, j] lies in group j, that is among blocks j * 8 to (j + 1) * 8 - 1. For each aligned block of 8 scenarios and each group, at most 3 of those scenarios link to one run of 2 blocks starting at a multiple of 2, and one such run has exactly 3.
All inputs are finite; a program needn't handle non-finite values. No bound on the sum of `pattern` on one device may be relied on, other than what follows from the above.
Results may differ from a plain program's by a relative error of at most 0.003.
Values may be sent and summed in bfloat16 or wider, within the bound.
No kernel may reach another device: no remote copies, remote signals or barrier semaphores. Data moves between devices by JAX's collectives and lax.ppermute only.
A program may use at most 128 MiB of HBM per device.

v0:
```python
import jax
import jax.numpy as jnp
from jax import lax
from jax.sharding import PartitionSpec as P


def on_device(factor_inv, pattern, border, row_scale, link_ids, first_diag):
    local_scen, scen_rows, _ = factor_inv.shape
    block_count = pattern.shape[1]
    block_size = border.shape[2]
    order_size = first_diag.shape[0]
    tile_count = lax.axis_size("tile")
    owner_count = lax.axis_size("scen")
    tile_id = lax.axis_index("tile")
    owner_id = lax.axis_index("scen")
    group_blocks = order_size // (tile_count * block_size)
    owner_blocks = order_size // (owner_count * block_size)
    owners_group = owner_count // tile_count
    capacity = local_scen // owners_group + local_scen // (2 * owners_group)
    index_blocks = jnp.arange(block_count)
    diagonal_mask = index_blocks[:, None] == index_blocks[None, :]
    below_diag = (index_blocks[:, None] > index_blocks[None, :]).astype(jnp.int32)
    effective = jnp.where(diagonal_mask[None], 1, pattern * below_diag[None])
    shaped = factor_inv.reshape(local_scen, block_count, block_size, block_count, block_size)
    masked = (shaped * effective[:, :, None, :, None].astype(jnp.bfloat16)).reshape(
        local_scen, scen_rows, scen_rows
    )
    solved_own = jnp.einsum(
        "snm,smc->snc", masked, border, preferred_element_type=jnp.float32
    ).astype(jnp.bfloat16)
    scaled = (row_scale[:, :, None] * solved_own.astype(jnp.float32)).astype(jnp.bfloat16)
    row_blocks = jnp.einsum(
        "snr,snc->src",
        scaled,
        lax.all_gather(solved_own, "tile", axis=2, tiled=True),
        preferred_element_type=jnp.float32,
    )
    blocks_out = jnp.transpose(
        row_blocks.reshape(local_scen, block_size, tile_count, block_size), (0, 2, 1, 3)
    )
    destination = link_ids // owner_blocks
    same_owner = destination[:, None, :] == destination[None, :, :]
    scen_index = jnp.arange(local_scen)
    earlier = (scen_index[None, :] < scen_index[:, None])[:, :, None]
    slot_rank = jnp.sum((same_owner & earlier).astype(jnp.int32), axis=1)
    own_links = lax.dynamic_slice_in_dim(link_ids, tile_id, 1, 1)[:, 0]
    row_local = own_links - tile_id * group_blocks
    target = row_local[:, None] * owner_blocks + link_ids % owner_blocks
    bin_count = group_blocks * owner_blocks
    send_blocks = jnp.zeros((owner_count, capacity, block_size, block_size), jnp.float32)
    send_blocks = send_blocks.at[destination, slot_rank].set(blocks_out)
    send_targets = jnp.full((owner_count, capacity), bin_count, jnp.int32)
    send_targets = send_targets.at[destination, slot_rank].set(target)
    received, received_targets = (
        lax.all_to_all(
            send_blocks.astype(jnp.bfloat16), "scen", split_axis=0, concat_axis=0, tiled=True
        ).astype(send_blocks.dtype),
        lax.all_to_all(send_targets, "scen", split_axis=0, concat_axis=0, tiled=True),
    )
    target_bins = jnp.zeros((bin_count + 1, block_size, block_size), jnp.float32)
    target_bins = target_bins.at[received_targets.reshape(-1)].add(
        received.reshape(-1, block_size, block_size)
    )
    tile_rows = group_blocks * block_size
    tile_cols = owner_blocks * block_size
    tile_out = jnp.transpose(
        target_bins[:bin_count].reshape(group_blocks, owner_blocks, block_size, block_size),
        (0, 2, 1, 3),
    ).reshape(tile_rows, tile_cols)
    row_start = tile_id * tile_rows
    col_start = owner_id * tile_cols
    global_rows = row_start + jnp.arange(tile_rows)
    global_cols = col_start + jnp.arange(tile_cols)
    diag_values = lax.dynamic_slice_in_dim(first_diag, row_start, tile_rows)
    on_diagonal = global_rows[:, None] == global_cols[None, :]
    return tile_out + jnp.where(on_diagonal, diag_values[:, None], 0.0)


def solution(mesh):
    in_specs = (
        P("scen", None, None),
        P("scen", None, None),
        P("scen", None, "tile"),
        P("scen", None),
        P("scen", None),
        P(),
    )
    out_specs = P("tile", "scen")
    return jax.shard_map(
        on_device, mesh=mesh, in_specs=in_specs, out_specs=out_specs, check_vma=False
    )
```

profile of v0, /device:TPU:25, one launch (start us, length us, event | category | flops | bytes accessed | tf_op | source)
XLA Modules:
  0.0 267.9 jit_solution(12266501531312780159)
XLA Ops:
  6.5 0.0 copy-start
  6.5 0.0 all-gather.2.cloned.1.call-start
  6.5 0.9 select_convert_fusion
  7.4 6.3 %mul.46 = bf16[8,6,128,6,128]{4,3,2,1,0:T(8,128)(2,1)} broadcast(bf16[8,6,6]{2,1,0:T(8,128)(2,1)S(1)} %copy.27), dimensions={0,1,3} | broadcast | bytes 9437760 | tf_op jit(solution)/shard_map/mul | solution.py:25
  13.7 20.4 %mul.47 = bf16[8,768,768]{2,1,0:T(8,128)(2,1)} reshape(bf16[8,6,128,6,128]{4,3,2,1,0:T(8,128)(2,1)} %mul.46) | data formatting | bytes 18874368 | tf_op jit(solution)/shard_map/mul | solution.py:25
  34.0 0.0 copy-done
  34.0 0.0 copy-start.4
  34.0 10.2 %fusion.2 = bf16[8,768,128]{2,1,0:T(8,128)(2,1)} fusion(bf16[8,768,128]{2,1,0:T(8,128)(2,1)S(1)} %copy-done, bf16[8,768,768]{2,1,0:T(8,128)(2,1)} %param.6, bf16[8,768,768]{2,1,0:T(8,128)(2,1)} %mul.47), kind=kOutput, calls=%fused_computation.9 | convolution fusion | flops 1213464576 | bytes 22020096 | tf_op jit(solution)/shard_map/snm,smc->snc/dot_general | solution.py:28
  44.2 0.0 all-gather.2.cloned.1.call-update
  44.3 0.0 copy-done.4
  44.3 0.2 multiply_reduce_fusion
  44.5 0.1 fusion.8
  44.5 0.1 convert_reduce_fusion
  44.6 0.1 reshape.125
  44.7 0.1 reshape.127
  44.8 0.0 copy-start.2
  44.8 0.0 copy-start.3
  44.8 3.5 %scatter_fusion = s32[32,3]{0,1:T(4,128)S(1)} fusion(s32[32,3]{0,1:T(4,128)S(1)} %broadcast_in_dim.29, s32[64]{0:T(128)S(1)} %reshape.125, s32[64]{0:T(128)S(1)} %reshape.127), kind=kCustom, calls=%fused_computation | custom fusion | bytes 1280 | tf_op jit(solution)/shard_map/scatter | solution.py:53
  48.3 0.7 copy.26
  49.0 10.9 %all-to-all-start = ((s32[32,1,3]{2,1,0:T(1,128)}), s32[32,1,3]{2,1,0:T(1,128)S(1)}, u32[]{:S(2)}, u32[]{:S(2)}) async-start(s32[32,1,3]{2,1,0:T(1,128)} %copy.26), calls=%async_computation | async-start | bytes 32768 | tf_op jit(solution)/shard_map/all_to_all | solution.py:58
  59.9 62.2 %all-gather.2.cloned.1.call-done = bf16[8,768,1024]{2,1,0:T(8,128)(2,1)} async-done(((bf16[8,768,128]{2,1,0:T(8,128)(2,1)}), bf16[8,768,1024]{2,1,0:T(8,128)(2,1)}) %all-gather.2.cloned.1.call-update) | async-done | bytes 12582928 | tf_op jit(solution)/shard_map/all_gather | solution.py:35
  122.2 0.0 copy-done.2
  122.2 0.0 copy-done.3
  122.2 6.3 %convolution_bitcast_fusion = f32[8,16,8,8,128]{4,3,2,1,0:T(8,128)S(1)} fusion(bf16[8,768,1024]{2,1,0:T(8,128)(2,1)} %all-gather.2.cloned.1.call-done, bf16[8,768,128]{2,1,0:T(8,128)(2,1)S(1)} %copy-done.2, f32[8,768]{1,0:T(8,128)S(1)} %copy-done.3), kind=kOutput, calls=%fused_computation.8 | convolution fusion | flops 1612972032 | bytes 18374656 | tf_op jit(solution)/shard_map/snr,snc->src/dot_general | solution.py:32
  128.5 2.6 copy.37
  131.1 3.4 %broadcast_in_dim.31 = f32[32,3,128,128]{3,2,1,0:T(8,128)} broadcast(f32[]{:T(128)} %constant.19.clone.1), dimensions={} | broadcast | bytes 6291460 | tf_op jit(solution)/shard_map/broadcast_in_dim | solution.py:50
  134.5 12.6 %scatter_fusion.1 = f32[32,3,128,128]{3,2,1,0:T(8,128)} fusion(f32[32,3,128,128]{3,2,1,0:T(8,128)} %broadcast_in_dim.31, s32[64]{0:T(128)S(1)} %reshape.125, f32[64,128,128]{2,1,0:T(8,128)} %bitcast.36), kind=kCustom, calls=%fused_computation.1 | custom fusion | bytes 12583424 | tf_op jit(solution)/shard_map/scatter | solution.py:51
  147.1 5.1 %convert_element_type.33 = bf16[32,3,128,128]{3,2,1,0:T(8,128)(2,1)} convert(f32[32,3,128,128]{3,2,1,0:T(8,128)} %scatter_fusion.1) | non-fusion elementwise | flops 1572864 | bytes 9437184 | tf_op jit(solution)/shard_map/convert_element_type | solution.py:56
  152.3 0.0 all-to-all-done
  152.3 9.7 %all-to-all-start.1 = ((bf16[32,3,128,128]{3,2,1,0:T(8,128)(2,1)}), bf16[32,3,128,128]{3,2,1,0:T(8,128)(2,1)}, u32[]{:S(2)}, u32[]{:S(2)}) async-start(bf16[32,3,128,128]{3,2,1,0:T(8,128)(2,1)} %convert_element_type.33), calls=%async_computation.1 | async-start | bytes 6291456 | tf_op jit(solution)/shard_map/all_to_all | solution.py:55
  162.0 0.5 broadcast.140
  162.5 0.7 reduce.5
  163.2 0.1 reshape.117
  163.3 72.8 %all-to-all-done.1 = bf16[32,3,128,128]{3,2,1,0:T(8,128)(2,1)} async-done(((bf16[32,3,128,128]{3,2,1,0:T(8,128)(2,1)}), bf16[32,3,128,128]{3,2,1,0:T(8,128)(2,1)}, u32[]{:S(2)}, u32[]{:S(2)}) %all-to-all-start.1) | async-done | bytes 3145760 | tf_op jit(solution)/shard_map/all_to_all | solution.py:55
  236.2 5.4 %bitcast_convert_fusion = f32[96,128,128]{2,1,0:T(8,128)} fusion(bf16[32,3,128,128]{3,2,1,0:T(8,128)(2,1)} %all-to-all-done.1), kind=kLoop, calls=%fused_computation.6 | loop fusion | flops 1572864 | bytes 9437184 | tf_op jit(solution)/shard_map/reshape | solution.py:62
  241.6 0.1 broadcast_in_dim.28
  241.7 0.0 copy-start.1
  241.7 12.9 %scatter_fusion.2 = f32[17,128,128]{2,1,0:T(8,128)S(1)} fusion(f32[17,128,128]{2,1,0:T(8,128)S(1)} %broadcast_in_dim.28, s32[96]{0:T(128)S(1)} %fusion.14, f32[96,128,128]{2,1,0:T(8,128)} %bitcast_convert_fusion), kind=kCustom, calls=%fused_computation.2 | custom fusion | flops 1572864 | bytes 18874752 | tf_op jit(solution)/shard_map/scatter-add | solution.py:61
  254.6 0.0 dynamic-slice-start
  254.6 1.0 slice.8
  255.7 1.6 copy.30
  257.3 0.0 dynamic-slice-done
  257.3 1.3 bitcast_add_fusion
  258.6 2.5 copy.31
  261.1 0.0 copy-done.1
  (8 shorter events, 0.0 us)
Async XLA Ops:
  6.5 27.5 %copy-start = (bf16[8,768,128]{2,1,0:T(8,128)(2,1)S(1)}, bf16[8,768,128]{2,1,0:T(8,128)(2,1)}, u32[]{:S(2)}) copy-start(bf16[8,768,128]{2,1,0:T(8,128)(2,1)} %param.8) | copy-start | bytes 4718596
  6.5 115.6 %all-gather.2.cloned.1.call-start = ((), (), s32[]{:S(2)}) async-start(), calls=%async_computation.2 | async-start | bytes 14155776 | tf_op jit(solution)/shard_map/all_gather | solution.py:35
  34.0 10.2 %copy-start.4 = (s32[8,8]{1,0:T(8,128)S(1)}, s32[8,8]{1,0:T(8,128)}, u32[]{:S(2)}) copy-start(s32[8,8]{1,0:T(8,128)} %param.10) | copy-start | bytes 772
  44.8 77.4 %copy-start.2 = (bf16[8,768,128]{2,1,0:T(8,128)(2,1)S(1)}, bf16[8,768,128]{2,1,0:T(8,128)(2,1)}, u32[]{:S(2)}) copy-start(bf16[8,768,128]{2,1,0:T(8,128)(2,1)} %fusion.2) | copy-start | bytes 4718596
  44.8 77.4 %copy-start.3 = (f32[8,768]{1,0:T(8,128)S(1)}, f32[8,768]{1,0:T(8,128)}, u32[]{:S(2)}) copy-start(f32[8,768]{1,0:T(8,128)} %param.9) | copy-start | bytes 73732
  49.0 103.2 %all-to-all-start = ((s32[32,1,3]{2,1,0:T(1,128)}), s32[32,1,3]{2,1,0:T(1,128)S(1)}, u32[]{:S(2)}, u32[]{:S(2)}) async-start(s32[32,1,3]{2,1,0:T(1,128)} %copy.26), calls=%async_computation | async-start | bytes 32768 | tf_op jit(solution)/shard_map/all_to_all | solution.py:58
  152.3 83.9 %all-to-all-start.1 = ((bf16[32,3,128,128]{3,2,1,0:T(8,128)(2,1)}), bf16[32,3,128,128]{3,2,1,0:T(8,128)(2,1)}, u32[]{:S(2)}, u32[]{:S(2)}) async-start(bf16[32,3,128,128]{3,2,1,0:T(8,128)(2,1)} %convert_element_type.33), calls=%async_computation.1 | async-start | bytes 6291456 | tf_op jit(solution)/shard_map/all_to_all | solution.py:55
  241.7 19.4 %copy-start.1 = (bf16[8,768,128]{2,1,0:T(8,128)(2,1)S(1)}, bf16[8,768,128]{2,1,0:T(8,128)(2,1)}, u32[]{:S(2)}) copy-start(bf16[8,768,128]{2,1,0:T(8,128)(2,1)} %param.8) | copy-start | bytes 4718596
  254.6 2.7 dynamic-slice-start
Sparse Core Ops, SparseCore 0:
  44.4 77.7 all-gather.1
where the time goes:
time: 269 us; the launch traced here: 268 us
  waiting for transfers between devices  135 us (50%)
  local copies, waits for them, and re-layouts  55.6 us (21%)
  other arithmetic  26.6 us (10%)
  starting transfers between devices  20.6 us (8%)
  matrix products  16.5 us (6%)
  between operations  13.6 us (5%)
    all_to_all x1, waiting for transfers between devices, on_device(): lax.all_to_all(send_blocks.astype(jnp.bfloat16), 'scen', split_axis=0, co...  72.8 us
    all_gather x1, waiting for transfers between devices, on_device(): lax.all_gather(solved_own, 'tile', axis=2, tiled=True)  62.2 us
    mul x2, local copies, waits for them, and re-layouts, on_device(): shaped * effective[:, :, None, :, None].astype(jnp.bfloat16)  26.6 us
    scatter-add x1, other arithmetic, on_device(): target_bins.at[received_targets.reshape(-1)]  12.9 us
    scatter x1, local copies, waits for them, and re-layouts, on_device(): send_blocks = send_blocks.at[destination, slot_rank].set(blocks_out)  12.6 us
    all_to_all x1, starting transfers between devices, on_device(): lax.all_to_all(send_targets, 'scen', split_axis=0, concat_axis=0, tiled=T...  10.9 us
    dot_general x1, matrix products, on_device(): jnp.einsum('snm,smc->snc', masked, border, preferred_element_type=jnp.flo...  10.2 us
    all_to_all x1, starting transfers between devices, on_device(): lax.all_to_all(send_blocks.astype(jnp.bfloat16), 'scen', split_axis=0, co...  9.71 us
  transfers between devices with their start and end apart: 3, of which 2 were waited for; matrix products, arithmetic and copies ran while one was open for 13% of the time, Pallas kernels for 0%

commit v1 on v0

--- a/solution.py
+++ b/solution.py
@@ -2,6 +2,13 @@
 import jax.numpy as jnp
 from jax import lax
 from jax.sharding import PartitionSpec as P
+
+
+def swapped_in(x, name, d):
+    count = lax.axis_size(name)
+    blocks = jnp.stack([x for _ in range(count)])
+    blocks = lax.all_to_all(blocks, name, split_axis=0, concat_axis=0)
+    return jnp.concatenate(blocks, axis=d)
 
 
 def on_device(factor_inv, pattern, border, row_scale, link_ids, first_diag):
@@ -32,7 +39,7 @@
     row_blocks = jnp.einsum(
         "snr,snc->src",
         scaled,
-        lax.all_gather(solved_own, "tile", axis=2, tiled=True),
+        swapped_in(solved_own, "tile", 2),
         preferred_element_type=jnp.float32,
     )
     blocks_out = jnp.transpose(

time: 269 us -> 340 us (1.26)
  waiting for transfers between devices: 135 us -> 206 us
  between operations: 13.6 us -> 0.17 us
  local copies, waits for them, and re-layouts: 55.6 us -> 63.3 us
  starting transfers between devices: 20.6 us -> 26.5 us
    all_to_all x0 -> x1, waiting for transfers between devices: none -> 134 us  [swapped_in(): blocks = lax.all_to_all(blocks, name, split_axis=0, concat_axis=0)]
    all_gather x1 -> x0, waiting for transfers between devices: 62.2 us -> none  [on_device(): lax.all_gather(solved_own, 'tile', axis=2, tiled=True)]
    another operation x0 -> x1, local copies, waits for them, and re-layouts: none -> 7.78 us  [swapped_in(): blocks = jnp.stack([x for _ in range(count)])]
    all_to_all x0 -> x1, starting transfers between devices: none -> 6.02 us  [swapped_in(): blocks = lax.all_to_all(blocks, name, split_axis=0, concat_axis=0)]
  transfers between devices with their start and end apart: 3 -> 3, of which waited for: 2 -> 2; matrix products, arithmetic and copies ran while one was open for 13% -> 11% of each run, Pallas kernels for 0% -> 0%
where the time goes in v1:
time: 340 us; the launch traced here: 337 us
  waiting for transfers between devices  206 us (61%)
  local copies, waits for them, and re-layouts  63.3 us (19%)
  other arithmetic  26.6 us (8%)
  starting transfers between devices  26.5 us (8%)
  matrix products  15.3 us (4%)
    all_to_all x1, waiting for transfers between devices, swapped_in(): blocks = lax.all_to_all(blocks, name, split_axis=0, concat_axis=0)  134 us
    all_to_all x1, waiting for transfers between devices, on_device(): lax.all_to_all(send_blocks.astype(jnp.bfloat16), 'scen', split_axis=0, co...  71.5 us
    mul x2, local copies, waits for them, and re-layouts, on_device(): shaped * effective[:, :, None, :, None].astype(jnp.bfloat16)  26.6 us
    scatter-add x1, other arithmetic, on_device(): target_bins.at[received_targets.reshape(-1)]  12.9 us
    scatter x1, local copies, waits for them, and re-layouts, on_device(): send_blocks = send_blocks.at[destination, slot_rank].set(blocks_out)  12.5 us
    all_to_all x1, starting transfers between devices, on_device(): lax.all_to_all(send_targets, 'scen', split_axis=0, concat_axis=0, tiled=T...  10.9 us
    all_to_all x1, starting transfers between devices, on_device(): lax.all_to_all(send_blocks.astype(jnp.bfloat16), 'scen', split_axis=0, co...  9.55 us
    dot_general x1, matrix products, on_device(): jnp.einsum('snm,smc->snc', masked, border, preferred_element_type=jnp.flo...  8.97 us
  transfers between devices with their start and end apart: 3, of which 2 were waited for; matrix products, arithmetic and copies ran while one was open for 11% of the time, Pallas kernels for 0%

profile of v1, /device:TPU:25, one launch (start us, length us, event | category | flops | bytes accessed | tf_op | source)
XLA Modules:
  0.0 337.3 jit_solution(8653709159066724900)
XLA Ops:
  0.0 0.0 copy-start
  0.0 0.9 select_convert_fusion
  0.9 6.3 %mul.46 = bf16[8,6,128,6,128]{4,3,2,1,0:T(8,128)(2,1)} broadcast(bf16[8,6,6]{2,1,0:T(8,128)(2,1)S(1)} %copy.28), dimensions={0,1,3} | broadcast | bytes 9437760 | tf_op jit(solution)/shard_map/mul | solution.py:32
  7.1 20.4 %mul.47 = bf16[8,768,768]{2,1,0:T(8,128)(2,1)} reshape(bf16[8,6,128,6,128]{4,3,2,1,0:T(8,128)(2,1)} %mul.46) | data formatting | bytes 18874368 | tf_op jit(solution)/shard_map/mul | solution.py:32
  27.5 0.0 copy-done
  27.5 9.0 %fusion.8 = bf16[8,768,128]{2,1,0:T(8,128)(2,1)S(1)} fusion(bf16[8,768,128]{2,1,0:T(8,128)(2,1)S(1)} %copy-done, bf16[8,768,768]{2,1,0:T(8,128)(2,1)} %param.6, bf16[8,768,768]{2,1,0:T(8,128)(2,1)} %mul.47), kind=kOutput, calls=%fused_computation.12 | convolution fusion | flops 1213464576 | bytes 22020096 | tf_op jit(solution)/shard_map/snm,smc->snc/dot_general | solution.py:35
  36.5 7.8 %stack.2 = bf16[8,8,768,128]{3,2,1,0:T(8,128)(2,1)} broadcast(bf16[8,768,128]{2,1,0:T(8,128)(2,1)S(1)} %fusion.8), dimensions={1,2,3} | broadcast | bytes 14155776 | tf_op jit(solution)/shard_map/stack | solution.py:9
  44.3 0.0 copy-start.2
  44.3 6.0 %all-to-all-start.1 = ((bf16[8,8,768,128]{3,2,1,0:T(8,128)(2,1)}), bf16[8,8,768,128]{3,2,1,0:T(8,128)(2,1)}, u32[]{:S(2)}, u32[]{:S(2)}) async-start(bf16[8,8,768,128]{3,2,1,0:T(8,128)(2,1)} %stack.2), calls=%async_computation.1 | async-start | bytes 25165824 | tf_op jit(solution)/shard_map/all_to_all | solution.py:10
  50.3 0.0 copy-done.2
  50.3 0.2 multiply_reduce_fusion
  50.5 0.1 fusion.14
  50.5 0.1 convert_reduce_fusion
  50.7 0.1 reshape.135
  50.7 0.1 reshape.137
  50.8 0.0 copy-start.3
  50.8 3.5 %scatter_fusion = s32[32,3]{0,1:T(4,128)S(1)} fusion(s32[32,3]{0,1:T(4,128)S(1)} %broadcast_in_dim.29, s32[64]{0:T(128)S(1)} %reshape.135, s32[64]{0:T(128)S(1)} %reshape.137), kind=kCustom, calls=%fused_computation | custom fusion | bytes 1280 | tf_op jit(solution)/shard_map/scatter | solution.py:60
  54.3 0.7 copy.27
  55.0 134.1 %all-to-all-done.1 = bf16[8,8,768,128]{3,2,1,0:T(8,128)(2,1)} async-done(((bf16[8,8,768,128]{3,2,1,0:T(8,128)(2,1)}), bf16[8,8,768,128]{3,2,1,0:T(8,128)(2,1)}, u32[]{:S(2)}, u32[]{:S(2)}) %all-to-all-start.1) | async-done | bytes 12582944 | tf_op jit(solution)/shard_map/all_to_all | solution.py:10
  189.1 10.9 %all-to-all-start = ((s32[32,1,3]{2,1,0:T(1,128)}), s32[32,1,3]{2,1,0:T(1,128)S(1)}, u32[]{:S(2)}, u32[]{:S(2)}) async-start(s32[32,1,3]{2,1,0:T(1,128)} %copy.27), calls=%async_computation | async-start | bytes 32768 | tf_op jit(solution)/shard_map/all_to_all | solution.py:65
  200.0 0.0 copy-done.3
  200.0 6.3 %fusion.5 = f32[8,16,8,8,128]{4,3,2,1,0:T(8,128)S(1)} fusion(bf16[8,768,128]{2,1,0:T(8,128)(2,1)S(1)} %fusion.8, f32[8,768]{1,0:T(8,128)S(1)} %copy-done.3, bf16[8,8,768,128]{3,2,1,0:T(8,128)(2,1)} %all-to-all-done.1), kind=kOutput, calls=%fused_computation.11 | convolution fusion | flops 1612972032 | bytes 18374656 | tf_op jit(solution)/shard_map/snr,snc->src/dot_general | solution.py:39
  206.3 2.6 copy.46
  208.9 3.4 %broadcast_in_dim.31 = f32[32,3,128,128]{3,2,1,0:T(8,128)} broadcast(f32[]{:T(128)} %constant.19.clone.1), dimensions={} | broadcast | bytes 6291460 | tf_op jit(solution)/shard_map/broadcast_in_dim | solution.py:57
  212.4 12.5 %scatter_fusion.1 = f32[32,3,128,128]{3,2,1,0:T(8,128)} fusion(f32[32,3,128,128]{3,2,1,0:T(8,128)} %broadcast_in_dim.31, s32[64]{0:T(128)S(1)} %reshape.135, f32[64,128,128]{2,1,0:T(8,128)} %bitcast.45), kind=kCustom, calls=%fused_computation.1 | custom fusion | bytes 12583424 | tf_op jit(solution)/shard_map/scatter | solution.py:58
  224.9 5.1 %convert_element_type.33 = bf16[32,3,128,128]{3,2,1,0:T(8,128)(2,1)} convert(f32[32,3,128,128]{3,2,1,0:T(8,128)} %scatter_fusion.1) | non-fusion elementwise | flops 1572864 | bytes 9437184 | tf_op jit(solution)/shard_map/convert_element_type | solution.py:63
  230.0 0.0 all-to-all-done
  230.0 9.6 %all-to-all-start.2 = ((bf16[32,3,128,128]{3,2,1,0:T(8,128)(2,1)}), bf16[32,3,128,128]{3,2,1,0:T(8,128)(2,1)}, u32[]{:S(2)}, u32[]{:S(2)}) async-start(bf16[32,3,128,128]{3,2,1,0:T(8,128)(2,1)} %convert_element_type.33), calls=%async_computation.2 | async-start | bytes 6291456 | tf_op jit(solution)/shard_map/all_to_all | solution.py:62
  239.6 0.5 broadcast.142
  240.1 0.7 reduce.5
  240.8 0.1 reshape.125
  240.9 71.5 %all-to-all-done.2 = bf16[32,3,128,128]{3,2,1,0:T(8,128)(2,1)} async-done(((bf16[32,3,128,128]{3,2,1,0:T(8,128)(2,1)}), bf16[32,3,128,128]{3,2,1,0:T(8,128)(2,1)}, u32[]{:S(2)}, u32[]{:S(2)}) %all-to-all-start.2) | async-done | bytes 3145760 | tf_op jit(solution)/shard_map/all_to_all | solution.py:62
  312.4 5.4 %bitcast_convert_fusion = f32[96,128,128]{2,1,0:T(8,128)} fusion(bf16[32,3,128,128]{3,2,1,0:T(8,128)(2,1)} %all-to-all-done.2), kind=kLoop, calls=%fused_computation.9 | loop fusion | flops 1572864 | bytes 9437184 | tf_op jit(solution)/shard_map/reshape | solution.py:69
  317.8 0.1 broadcast_in_dim.28
  317.9 0.0 copy-start.1
  317.9 12.9 %scatter_fusion.2 = f32[17,128,128]{2,1,0:T(8,128)S(1)} fusion(f32[17,128,128]{2,1,0:T(8,128)S(1)} %broadcast_in_dim.28, s32[96]{0:T(128)S(1)} %fusion.20, f32[96,128,128]{2,1,0:T(8,128)} %bitcast_convert_fusion), kind=kCustom, calls=%fused_computation.2 | custom fusion | flops 1572864 | bytes 18874752 | tf_op jit(solution)/shard_map/scatter-add | solution.py:68
  330.8 0.0 dynamic-slice-start
  330.8 1.0 slice.8
  331.9 1.6 copy.32
  333.5 0.0 dynamic-slice-done
  333.5 1.3 bitcast_add_fusion
  334.8 2.5 copy.33
  337.3 0.0 copy-done.1
  (8 shorter events, 0.0 us)
Async XLA Ops:
  0.0 27.5 %copy-start = (bf16[8,768,128]{2,1,0:T(8,128)(2,1)S(1)}, bf16[8,768,128]{2,1,0:T(8,128)(2,1)}, u32[]{:S(2)}) copy-start(bf16[8,768,128]{2,1,0:T(8,128)(2,1)} %param.8) | copy-start | bytes 4718596
  44.3 6.0 %copy-start.2 = (s32[8,8]{1,0:T(8,128)S(1)}, s32[8,8]{1,0:T(8,128)}, u32[]{:S(2)}) copy-start(s32[8,8]{1,0:T(8,128)} %param.10) | copy-start | bytes 772
  44.3 144.8 %all-to-all-start.1 = ((bf16[8,8,768,128]{3,2,1,0:T(8,128)(2,1)}), bf16[8,8,768,128]{3,2,1,0:T(8,128)(2,1)}, u32[]{:S(2)}, u32[]{:S(2)}) async-start(bf16[8,8,768,128]{3,2,1,0:T(8,128)(2,1)} %stack.2), calls=%async_computation.1 | async-start | bytes 25165824 | tf_op jit(solution)/shard_map/all_to_all | solution.py:10
  50.8 149.2 %copy-start.3 = (f32[8,768]{1,0:T(8,128)S(1)}, f32[8,768]{1,0:T(8,128)}, u32[]{:S(2)}) copy-start(f32[8,768]{1,0:T(8,128)} %param.9) | copy-start | bytes 73732
  189.1 40.9 %all-to-all-start = ((s32[32,1,3]{2,1,0:T(1,128)}), s32[32,1,3]{2,1,0:T(1,128)S(1)}, u32[]{:S(2)}, u32[]{:S(2)}) async-start(s32[32,1,3]{2,1,0:T(1,128)} %copy.27), calls=%async_computation | async-start | bytes 32768 | tf_op jit(solution)/shard_map/all_to_all | solution.py:65
  230.0 82.4 %all-to-all-start.2 = ((bf16[32,3,128,128]{3,2,1,0:T(8,128)(2,1)}), bf16[32,3,128,128]{3,2,1,0:T(8,128)(2,1)}, u32[]{:S(2)}, u32[]{:S(2)}) async-start(bf16[32,3,128,128]{3,2,1,0:T(8,128)(2,1)} %convert_element_type.33), calls=%async_computation.2 | async-start | bytes 6291456 | tf_op jit(solution)/shard_map/all_to_all | solution.py:62
  317.9 19.4 %copy-start.1 = (bf16[8,768,128]{2,1,0:T(8,128)(2,1)S(1)}, bf16[8,768,128]{2,1,0:T(8,128)(2,1)}, u32[]{:S(2)}) copy-start(bf16[8,768,128]{2,1,0:T(8,128)(2,1)} %param.8) | copy-start | bytes 4718596
  330.8 2.7 dynamic-slice-start
